TPU v7x, 32 devices: a whole 2x2x4 slice. The times are simulated.
32 devices in a mesh: dp: 8 (over y, x, core), space: 4 (over z).
Axes of the slice: x: 2, y: 2, z: 4, core: 2. Of those that a mesh axis runs over, the one named last changes fastest.
Arguments:
- features: bfloat16 [8, 32, 16, 512], P('dp', 'space'), may hold values from -48 to 48
- cotangent: bfloat16 [8, 32, 16, 512], P('dp', 'space'), may hold values from -6 to 6
- dw_kernel: float32 [7, 7, 512], replicated, may hold values from -0.875 to 0.875
- ln_gain: float32 [512], replicated, may hold values from 0.1 to 1.9
- ln_bias: float32 [512], replicated, may hold values from -3 to 3
- layer_scale: float32 [512], replicated, may hold values from 0.3 to 3
- w_up: bfloat16 [512, 2048], P('dp'), may hold values from -0.25 to 0.25
- w_down: bfloat16 [2048, 512], P('dp'), may hold values from -0.125 to 0.125
Outputs:
- result: bfloat16 [8, 32, 16, 512], P('dp', 'space')
- d_features: float32 [8, 32, 16, 512], P('dp', 'space')
- d_w_up: float32 [512, 2048], P('dp', 'space')
- d_w_down: float32 [2048, 512], P('space', 'dp')
- d_kernel: float32 [7, 7, 512], replicated
- d_gain: float32 [512], replicated
- d_bias: float32 [512], replicated
- d_scale: float32 [512], replicated
All inputs are finite; a program needn't handle non-finite values.
Results may differ from a plain program's by a relative error of at most 0.0065.
Values may be sent and summed in bfloat16 or wider, within the bound.
A program may use at most 64 MiB of HBM per device.

v0:
```python
import functools
import math

import jax
import jax.numpy as jnp
from jax import lax
from jax.experimental import pallas as pl
from jax.experimental.pallas import tpu as pltpu
from jax.sharding import PartitionSpec as P

F32, BF16 = jnp.float32, jnp.bfloat16
LANES = 128
EDGE = 8


def gelu_pair(preact):
    cumulative = 0.5 * (1.0 + lax.erf(preact * (1.0 / math.sqrt(2.0))))
    density = jnp.exp(-0.5 * preact * preact) * (1.0 / math.sqrt(2.0 * math.pi))
    return (preact * cumulative, cumulative + preact * density)


def remote(src, dst, send_sem, recv_sem, device):
    return pltpu.make_async_remote_copy(
        src_ref=src,
        dst_ref=dst,
        send_sem=send_sem,
        recv_sem=recv_sem,
        device_id=device,
        device_id_type=pl.DeviceIdType.MESH,
    )


def block_kernel(
    sizes,
    x_ref, cot_ref, kern_ref, gain_ref, bias_ref, scale_ref, wup_ref, wdown_ref,
    res_ref, dfeat_ref, gup_ref, gdown_ref, gkern_ref, ggain_ref, gbias_ref, gscale_ref,
    xpad, gpad, halo_x, halo_g, conv, scaled_ref, dconv, wout, upg, tok, dmx, hid, dpre,
    part_n, part_m, r1n, r1m, chip_n, chip_m, r2n, r2m, own_n, own_m,
    gpart, gsend, grecv, fsend, frecv, dscale, small, ar1, ar2, ar3,
    hx_s, hx_r, hg_s, hg_r, w_s, w_r, dm_s, dm_r, tk_s, tk_r,
    an_s, an_r, am_s, am_r, bn_s, bn_r, bm_s, bm_r,
    gz_s, gz_r, fi_s, fi_r, s1_s, s1_r, s2_s, s2_r, s3_s, s3_r,
):
    n_dp, n_sp, rows, cols, width, taps = sizes
    chips, share = n_dp // 2, n_dp // n_sp
    margin = taps // 2
    pixels = rows * cols
    hidden = wdown_ref.shape[0]
    d, s = lax.axis_index("dp"), lax.axis_index("space")
    chip, core = d // 2, lax.rem(d, 2)
    sibling = chip * 2 + (1 - core)
    home = d // share
    place = lax.rem(d, share)
    inside = (home == s).astype(jnp.int32)

    def is_self(b):
        return jnp.logical_and(home == s, place == b)

    def dp_peer(off):
        return lax.rem(d + off, n_dp)

    def sp_peer(off):
        return lax.rem(s + off, n_sp)

    barrier = pltpu.get_barrier_semaphore()

    def greet(device):
        pl.semaphore_signal(barrier, inc=1, device_id=device, device_id_type=pl.DeviceIdType.MESH)

    for off in range(1, n_dp):
        greet((dp_peer(off), s))
    for off in range(1, n_sp):
        greet((d, sp_peer(off)))
    for b in range(share):
        @pl.when(jnp.logical_not(is_self(b)))
        def _():
            greet((s * share + b, home))

    dmx[d] = (scale_ref[...] * cot_ref[...].astype(F32)).astype(BF16)
    for t in range(n_dp):
        wout[t] = wup_ref[:, t * hidden:(t + 1) * hidden]
    upg[d] = wout[d]
    for padded in (xpad, gpad):
        padded[...] = jnp.zeros(padded.shape, F32)
    xpad[margin:margin + rows, EDGE:EDGE + cols] = x_ref[...].astype(F32)
    dscale[...] = jnp.zeros(dscale.shape, F32)
    small[...] = jnp.zeros(small.shape, F32)
    pl.semaphore_wait(barrier, (n_dp - 1) + (n_sp - 1) + share - inside)

    has_up, has_down = s > 0, s < n_sp - 1

    def halo_copies(source, halo, send, recv):
        down = remote(source.at[pl.ds(rows - margin, margin)], halo.at[0], send.at[0], recv.at[0], (d, jnp.minimum(s + 1, n_sp - 1)))
        up = remote(source.at[pl.ds(0, margin)], halo.at[1], send.at[1], recv.at[1], (d, jnp.maximum(s - 1, 0)))
        return down, up

    def halo_start(copies):
        pl.when(has_down)(copies[0].start)
        pl.when(has_up)(copies[1].start)

    def halo_land(copies, halo, padded):
        @pl.when(has_up)
        def _():
            copies[0].wait_recv()
            padded[0:margin, EDGE:EDGE + cols] = halo[0].astype(F32)

        @pl.when(has_down)
        def _():
            copies[1].wait_recv()
            padded[rows + margin:, EDGE:EDGE + cols] = halo[1].astype(F32)

    def halo_sent(copies):
        pl.when(has_down)(copies[0].wait_send)
        pl.when(has_up)(copies[1].wait_send)

    hx = halo_copies(x_ref, halo_x, hx_s, hx_r)
    halo_start(hx)

    def spread(buf, send, recv):
        first = [remote(buf.at[d], buf.at[d], send.at[0], recv.at[d], (sibling, s))]
        for off in range(1, chips):
            first.append(remote(buf.at[d], buf.at[d], send.at[off], recv.at[d], (lax.rem(chip + off, chips) * 2 + core, s)))
        passed = []
        for off in range(1, chips):
            slot = lax.rem(chip + chips - off, chips) * 2 + core
            passed.append(remote(buf.at[slot], buf.at[slot], send.at[chips - 1 + off], recv.at[slot], (sibling, s)))
        last = []
        for off in range(chips):
            slot = lax.rem(chip + chips - off, chips) * 2 + (1 - core)
            last.append(remote(buf.at[slot], buf.at[slot], send.at[0], recv.at[slot], (sibling, s)))
        return first, passed, last

    dm_first, dm_passed, dm_last = spread(dmx, dm_s, dm_r)
    w_out = [remote(wout.at[dp_peer(off)], upg.at[d], w_s.at[off], w_r.at[d], (dp_peer(off), s)) for off in range(1, n_dp)]
    w_in = [remote(wout.at[dp_peer(off)], upg.at[dp_peer(off)], w_s.at[off], w_r.at[dp_peer(off)], (sibling, s)) for off in range(1, n_dp)]
    for copy in w_out:
        copy.start()
    for copy in dm_first:
        copy.start()

    halo_land(hx, halo_x, xpad)

    def convolve(padded, flip, lanes):
        total = jnp.zeros((rows, cols, LANES), F32)
        for b in range(taps):
            first = EDGE - margin + b
            window = padded[:, first:first + cols, lanes]
            for a in range(taps):
                at = (taps - 1 - a, taps - 1 - b) if flip else (a, b)
                tap = kern_ref[at[0], at[1]:at[1] + 1, lanes].reshape(1, 1, LANES)
                total = total + tap * window[a:a + rows]
        return total

    def lanes_of(c):
        return pl.ds(pl.multiple_of(c * LANES, LANES), LANES)

    @pl.loop(0, width // LANES)
    def _(c):
        conv[:, lanes_of(c)] = convolve(xpad, False, lanes_of(c)).reshape(pixels, LANES)

    center = conv[...]
    center = center - jnp.mean(center, axis=-1, keepdims=True)
    inverse = lax.rsqrt(jnp.mean(center * center, axis=-1, keepdims=True) + 1e-06)
    normal = center * inverse
    scaled_ref[...] = normal
    tok[d] = (normal * gain_ref[...] + bias_ref[...]).astype(BF16)

    tk_first, tk_passed, tk_last = spread(tok, tk_s, tk_r)
    for copy in tk_first:
        copy.start()
    for group in (dm_passed, tk_passed):
        for copy in group:
            copy.wait_recv()
            copy.start()
    for copy in w_in:
        copy.wait_recv()
    for group in (dm_last, tk_last):
        for copy in group:
            copy.wait_recv()

    def nn(a, b):
        return lax.dot_general(a, b, (((1,), (0,)), ((), ())), preferred_element_type=F32)

    def nt(a, b):
        return lax.dot_general(a, b, (((1,), (1,)), ((), ())), preferred_element_type=F32)

    def tn(a, b):
        return lax.dot_general(a, b, (((0,), (0,)), ((), ())), preferred_element_type=F32)

    def cross(kind, to):
        buf, got, send, recv = kind
        return remote(buf.at[to], got.at[to], send.at[to], recv.at[to], (sibling, s))

    def home_copy(kind, to):
        buf, got, send, recv = kind
        return remote(buf.at[to], got.at[chip], send.at[to], recv.at[chip], (to * 2 + core, s))

    cross_n, cross_m = (part_n, r1n, an_s, an_r), (part_m, r1m, am_s, am_r)
    home_n, home_m = (chip_n, r2n, bn_s, bn_r), (chip_m, r2m, bm_s, bm_r)

    def products(slot):
        up = upg[...].reshape(width, hidden)
        activation, slope = gelu_pair(nn(tok[slot], up))
        act = activation.astype(BF16)
        grad = (nt(dmx[slot], wdown_ref[...]) * slope).astype(BF16)
        hid[slot] = act
        dpre[slot] = grad
        mixed = nn(act, wdown_ref[...])
        dscale[...] += jnp.sum(dmx[slot].astype(F32) * mixed, axis=0, keepdims=True)
        return nt(grad, up), mixed

    @pl.loop(0, chips)
    def _(i):
        to = lax.rem(chip + 1 + i, chips)
        normed, mixed = products(to * 2 + (1 - core))
        part_n[to] = normed.astype(BF16)
        cross(cross_n, to).start()
        part_m[to] = mixed.astype(BF16)
        cross(cross_m, to).start()

    @pl.loop(0, chips - 1)
    def _(i):
        to = lax.rem(chip + 1 + i, chips)
        normed, mixed = products(to * 2 + core)
        cross(cross_n, to).wait_recv()
        chip_n[to] = (normed + r1n[to].astype(F32)).astype(BF16)
        home_copy(home_n, to).start()
        cross(cross_m, to).wait_recv()
        chip_m[to] = (mixed + r1m[to].astype(F32)).astype(BF16)

    normed, mixed = products(d)
    cross(cross_n, chip).wait_recv()
    own_n[...] = normed + r1n[chip].astype(F32)
    cross(cross_m, chip).wait_recv()
    own_m[...] = mixed + r1m[chip].astype(F32)

    strip = width // n_sp
    part_rows = strip // share
    flat = (n_dp * pixels,)

    def plane_copy(which, off, landing):
        to = sp_peer(off)
        slot = to if landing else s
        return remote(gsend.at[which, to], grecv.at[which, slot], gz_s.at[which, off], gz_r.at[which, slot], (d, to))

    for which, (left, right) in enumerate(((tok, dpre), (dmx, hid))):
        gpart[which] = tn(left[...].reshape(flat + (width,)), right[...].reshape(flat + (hidden,)))
        for k in range(n_sp):
            gsend[which, k] = gpart[which, k * strip:(k + 1) * strip].astype(BF16)
        for off in range(1, n_sp):
            plane_copy(which, off, False).start()

    def arrive(got, send, recv, own):
        total = own[...]
        for off in range(1, chips):
            source = lax.rem(chip + off, chips)
            remote(got.at[source], got.at[source], send.at[source], recv.at[source], (sibling, s)).wait_recv()
            total = total + got[source].astype(F32)
        return total

    d_norm = arrive(r2n, bn_s, bn_r, own_n)
    for off in range(1, chips):
        home_copy(home_m, lax.rem(chip + off, chips)).start()
    normal = scaled_ref[...]
    d_hat = d_norm * gain_ref[...]
    lead = jnp.mean(d_hat, axis=-1, keepdims=True)
    second = jnp.mean(d_hat * normal, axis=-1, keepdims=True)
    dconv[...] = (inverse * (d_hat - lead - normal * second)).astype(BF16).reshape(rows, cols, width)
    hg = halo_copies(dconv, halo_g, hg_s, hg_r)
    halo_start(hg)
    gpad[margin:margin + rows, EDGE:EDGE + cols] = dconv[...].astype(F32)

    per = small.shape[1]
    count = taps * taps

    def put(row, lanes, value):
        small[row // per, row % per:row % per + 1, lanes] = value

    everything = slice(None)
    put(count, everything, jnp.sum(d_norm * normal, axis=0, keepdims=True))
    put(count + 1, everything, jnp.sum(d_norm, axis=0, keepdims=True))
    put(count + 2, everything, dscale[...] / scale_ref[...])

    @pl.loop(0, width // LANES)
    def _(c):
        lanes = lanes_of(c)
        upstream = gpad[margin:margin + rows, EDGE:EDGE + cols, lanes]
        for b in range(taps):
            first = EDGE - margin + b
            window = xpad[:, first:first + cols, lanes]
            for a in range(taps):
                product = jnp.sum(window[a:a + rows] * upstream, axis=0)
                put(a * taps + b, lanes, jnp.sum(product, axis=0, keepdims=True))

    s1_out = [remote(small.at[dp_peer(off)], ar1.at[d], s1_s.at[off], s1_r.at[d], (dp_peer(off), s)) for off in range(1, n_dp)]
    s1_in = [remote(small.at[dp_peer(off)], ar1.at[dp_peer(off)], s1_s.at[off], s1_r.at[dp_peer(off)], (sibling, s)) for off in range(1, n_dp)]
    for copy in s1_out:
        copy.start()
    ar1[d] = small[d]

    halo_land(hg, halo_g, gpad)

    @pl.loop(0, width // LANES)
    def _(c):
        lanes = lanes_of(c)
        cot = cot_ref[:, lanes].astype(F32).reshape(rows, cols, LANES)
        dfeat_ref[:, :, lanes] = cot + convolve(gpad, True, lanes)

    for copy in s1_in:
        copy.wait_recv()
    ar2[s] = jnp.sum(ar1[...], axis=0)
    s2_out = [remote(ar2.at[s], ar2.at[s], s2_s.at[off], s2_r.at[s], (d, sp_peer(off))) for off in range(1, n_sp)]
    s2_in = [remote(ar2.at[s], ar2.at[sp_peer(off)], s2_s.at[off], s2_r.at[sp_peer(off)], (d, sp_peer(off))) for off in range(1, n_sp)]
    for copy in s2_out:
        copy.start()

    def owner_copy(which, b):
        return remote(fsend.at[which, b], frecv.at[which, place], fi_s.at[which, b], fi_r.at[which, place], (s * share + b, home))

    for which in range(2):
        total = gpart[which, pl.ds(pl.multiple_of(s * strip, strip), strip)]
        for off in range(1, n_sp):
            plane_copy(which, off, True).wait_recv()
            total = total + grecv[which, sp_peer(off)].astype(F32)
        for b in range(share):
            fsend[which, b] = total[b * part_rows:(b + 1) * part_rows].astype(BF16)
            pl.when(jnp.logical_not(is_self(b)))(owner_copy(which, b).start)

            @pl.when(is_self(b))
            def _():
                frecv[which, b] = fsend[which, b]

    mixed = arrive(r2m, bm_s, bm_r, own_m)
    res_ref[...] = (x_ref[...].reshape(pixels, width).astype(F32) + scale_ref[...] * mixed).astype(BF16).reshape(rows, cols, width)

    for copy in s2_in:
        copy.wait_recv()
    ar3[d] = jnp.sum(ar2[...], axis=0)
    s3_out = [remote(ar3.at[d], ar3.at[d], s3_s.at[off], s3_r.at[d], (dp_peer(off), s)) for off in range(1, n_dp)]
    s3_in = [remote(ar3.at[d], ar3.at[dp_peer(off)], s3_s.at[off], s3_r.at[dp_peer(off)], (sibling, s)) for off in range(1, n_dp)]
    for copy in s3_out:
        copy.start()

    for which, out in enumerate((gup_ref, gdown_ref)):
        for b in range(share):
            landed = remote(fsend.at[which, b], frecv.at[which, b], fi_s.at[which, b], fi_r.at[which, b], (sibling, s))
            pl.when(jnp.logical_not(is_self(b)))(landed.wait_recv)
        for b in range(share):
            out[:, b * hidden:(b + 1) * hidden] = frecv[which, b].astype(F32)

    for copy in s3_in:
        copy.wait_recv()

    def take(row):
        return ar3[row // per, row % per:row % per + 1]

    for a in range(taps):
        for b in range(taps):
            gkern_ref[a, b:b + 1] = take(a * taps + b)
    ggain_ref[...] = take(count)
    gbias_ref[...] = take(count + 1)
    gscale_ref[...] = take(count + 2)

    halo_sent(hx)
    halo_sent(hg)
    for group in (w_out, dm_first, dm_passed, tk_first, tk_passed, s1_out, s2_out, s3_out):
        for copy in group:
            copy.wait_send()
    for which in range(2):
        for off in range(1, n_sp):
            plane_copy(which, off, False).wait_send()
        for b in range(share):
            pl.when(jnp.logical_not(is_self(b)))(owner_copy(which, b).wait_send)

    for off in range(chips):
        to = lax.rem(chip + 1 + off, chips)
        cross(cross_n, to).wait_send()
        cross(cross_m, to).wait_send()
        if off < chips - 1:
            home_copy(home_n, to).wait_send()
            home_copy(home_m, to).wait_send()


def local(features, cotangent, dw_kernel, ln_gain, ln_bias, layer_scale, w_up, w_down):
    n_dp, n_sp = lax.axis_size("dp"), lax.axis_size("space")
    _, rows, cols, width = features.shape
    taps = dw_kernel.shape[0]
    margin = taps // 2
    pixels = rows * cols
    hidden = w_down.shape[0]
    chips, share = n_dp // 2, n_dp // n_sp
    strip = width // n_sp
    part_rows = strip // share
    count = taps * taps
    per = -(-(count + 3) // n_dp)
    blocks = (n_dp, w_up.shape[0], hidden)
    padded = (rows + 2 * margin, cols + 2 * EDGE, width)
    dma = lambda k: pltpu.SemaphoreType.DMA((k,))
    vm = pltpu.VMEM
    scratch = [
        vm(padded, F32), vm(padded, F32),
        vm((2, margin, cols, width), BF16), vm((2, margin, cols, width), BF16),
        vm((pixels, width), F32), vm((pixels, width), F32), vm((rows, cols, width), BF16),
        vm(blocks, BF16), vm(blocks, BF16),
        vm((n_dp, pixels, width), BF16), vm((n_dp, pixels, width), BF16),
        vm((n_dp, pixels, hidden), BF16), vm((n_dp, pixels, hidden), BF16),
    ]
    scratch += [vm((chips, pixels, width), BF16)] * 8
    scratch += [vm((pixels, width), F32)] * 2
    scratch += [
        vm((2, width, hidden), F32),
        vm((2, n_sp, strip, hidden), BF16), vm((2, n_sp, strip, hidden), BF16),
        vm((2, share, part_rows, hidden), BF16), vm((2, share, part_rows, hidden), BF16),
        vm((1, width), F32),
        vm((n_dp, per, width), F32), vm((n_dp, per, width), F32),
        vm((n_sp, per, width), F32), vm((n_dp, per, width), F32),
    ]
    scratch += [dma(2)] * 4 + [dma(n_dp)] * 6 + [dma(chips)] * 8
    pair = lambda k: pltpu.SemaphoreType.DMA((2, k))
    scratch += [pair(n_sp)] * 2 + [pair(share)] * 2 + [dma(n_dp)] * 2 + [dma(n_sp)] * 2 + [dma(n_dp)] * 2
    whole = pl.BlockSpec(memory_space=pltpu.VMEM)
    result, d_feat, grad_up, grad_down, kernel_sum, gain_sum, bias_sum, scale_sum = pl.pallas_call(
        functools.partial(block_kernel, (n_dp, n_sp, rows, cols, width, taps)),
        out_shape=(
            jax.ShapeDtypeStruct((rows, cols, width), BF16),
            jax.ShapeDtypeStruct((rows, cols, width), F32),
            jax.ShapeDtypeStruct((part_rows, share * hidden), F32),
            jax.ShapeDtypeStruct((part_rows, share * hidden), F32),
            jax.ShapeDtypeStruct((taps, taps, width), F32),
        )
        + (jax.ShapeDtypeStruct((1, width), F32),) * 3,
        in_specs=[whole] * 8,
        out_specs=(whole,) * 8,
        scratch_shapes=scratch,
        compiler_params=pltpu.CompilerParams(
            collective_id=0, has_side_effects=True, vmem_limit_bytes=60 << 20
        ),
    )(
        features[0],
        cotangent[0].reshape(pixels, width),
        dw_kernel,
        ln_gain.reshape(1, width),
        ln_bias.reshape(1, width),
        layer_scale.reshape(1, width),
        w_up,
        w_down,
    )
    regions = float(n_dp)
    return (
        result[None],
        d_feat[None],
        grad_up / regions,
        grad_down.T / regions,
        kernel_sum / regions,
        gain_sum[0] / regions,
        bias_sum[0] / regions,
        scale_sum[0] / regions,
    )


def solution(mesh):
    in_specs = (
        P("dp", "space", None, None),
        P("dp", "space", None, None),
        P(),
        P(),
        P(),
        P(),
        P("dp", None),
        P("dp", None),
    )
    out_specs = (
        P("dp", "space", None, None),
        P("dp", "space", None, None),
        P("dp", "space"),
        P("space", "dp"),
        P(),
        P(),
        P(),
        P(),
    )
    return jax.shard_map(local, mesh=mesh, in_specs=in_specs, out_specs=out_specs, check_vma=False)
```

profile of v0, /device:TPU:3, one launch (start us, length us, event | category | flops | bytes accessed | tf_op | source)
XLA Modules:
  0.0 63.6 jit_solution(5788348516922951866)
XLA Ops:
  0.6 57.2 %shard_map.143 = (bf16[8,16,512]{2,1,0:T(8,128)(2,1)}, f32[8,16,512]{2,1,0:T(8,128)}, f32[64,512]{1,0:T(8,128)}, f32[64,512]{1,0:T(8,128)}, f32[7,7,512]{2,1,0:T...) custom-call(bf16[8,16,512]{2,1,0:T(8,128)(2,1)} %bitcast.13, bf16[128,512]{1,0:T(8,128)(2,1)} %bitcast.14, ...), custom_call_target="tpu_custom_call" | custom-call | tf_op jit(solution)/shard_map/pallas_call | solution.py:422
  57.8 0.0 copy-start.6
  57.8 0.0 copy-start.5
  57.8 0.0 copy-start.4
  57.8 0.0 copy-start.2
  57.9 0.0 copy-start.3
  57.9 0.6 %copy-done.4 = f32[1,512]{1,0:T(1,128)S(1)} copy-done((f32[1,512]{1,0:T(1,128)S(1)}, f32[1,512]{1,0:T(1,128)}, u32[]{:S(2)}) %copy-start.4) | copy-done | bytes 2072
  58.5 0.6 broadcast_multiply_fusion.4
  59.1 0.0 copy-done.6
  59.1 0.0 copy-done.5
  59.1 0.6 broadcast_multiply_fusion.2
  59.7 1.6 %broadcast_multiply_fusion.1 = f32[7,7,512]{2,1,0:T(8,128)} fusion(f32[7,7,512]{2,1,0:T(8,128)} %get-tuple-element.20), kind=kLoop, calls=%fused_computation.2 | loop fusion | flops 25088 | bytes 200704 | tf_op jit(solution)/shard_map/div | solution.py:454
  61.2 0.0 copy-done.2
  61.2 0.0 copy-done.3
  61.2 0.0 copy-start.1
  61.2 0.7 %multiply_bitcast_fusion = (f32[512,64]{0,1:T(8,128)}, f32[64,512]{1,0:T(8,128)}) fusion(f32[64,512]{1,0:T(8,128)S(1)} %copy-done.3, f32[64,512]{1,0:T(8,128)S(1)} %copy-done.2), kind=kLoop, calls=%fused_computation | loop fusion | flops 65536 | bytes 524288 | tf_op jit(solution)/shard_map/div | solution.py:453
  62.0 0.0 copy-start
  62.0 0.2 copy-done.1
  62.2 0.7 %copy.18 = bf16[1,8,16,512]{3,2,1,0:T(8,128)(2,1)} copy(bf16[1,8,16,512]{3,2,1,0:T(8,128)(2,1)S(1)} %bitcast.15) | data formatting | bytes 262144
  62.9 0.1 copy-done
  62.9 0.7 %copy.19 = f32[1,8,16,512]{3,2,1,0:T(8,128)} copy(f32[1,8,16,512]{3,2,1,0:T(8,128)S(1)} %bitcast.12) | data formatting | bytes 524288
Async XLA Ops:
  57.8 1.3 %copy-start.6 = (f32[1,512]{1,0:T(1,128)S(1)}, f32[1,512]{1,0:T(1,128)}, u32[]{:S(2)}) copy-start(f32[1,512]{1,0:T(1,128)} %get-tuple-element.23) | copy-start | bytes 6148
  57.8 1.3 %copy-start.5 = (f32[1,512]{1,0:T(1,128)S(1)}, f32[1,512]{1,0:T(1,128)}, u32[]{:S(2)}) copy-start(f32[1,512]{1,0:T(1,128)} %get-tuple-element.22) | copy-start | bytes 6148
  57.8 0.7 %copy-start.4 = (f32[1,512]{1,0:T(1,128)S(1)}, f32[1,512]{1,0:T(1,128)}, u32[]{:S(2)}) copy-start(f32[1,512]{1,0:T(1,128)} %get-tuple-element.21) | copy-start | bytes 6148
  57.8 3.4 %copy-start.2 = (f32[64,512]{1,0:T(8,128)S(1)}, f32[64,512]{1,0:T(8,128)}, u32[]{:S(2)}) copy-start(f32[64,512]{1,0:T(8,128)} %get-tuple-element.18) | copy-start | bytes 393220
  57.9 3.4 %copy-start.3 = (f32[64,512]{1,0:T(8,128)S(1)}, f32[64,512]{1,0:T(8,128)}, u32[]{:S(2)}) copy-start(f32[64,512]{1,0:T(8,128)} %get-tuple-element.19) | copy-start | bytes 393220
  61.2 1.0 %copy-start.1 = (bf16[8,16,512]{2,1,0:T(8,128)(2,1)S(1)}, bf16[8,16,512]{2,1,0:T(8,128)(2,1)}, u32[]{:S(2)}) copy-start(bf16[8,16,512]{2,1,0:T(8,128)(2,1)} %get-tuple-element.16) | copy-start | bytes 393220
  62.0 1.0 %copy-start = (f32[8,16,512]{2,1,0:T(8,128)S(1)}, f32[8,16,512]{2,1,0:T(8,128)}, u32[]{:S(2)}) copy-start(f32[8,16,512]{2,1,0:T(8,128)} %get-tuple-element.17) | copy-start | bytes 786436
where the time goes:
time: 63.8 us; the launch traced here: 63.6 us
  Pallas kernels  57.2 us (90%)
  other arithmetic  3.44 us (5%)
  local copies, waits for them, and re-layouts  2.33 us (4%)
  between operations  0.69 us (1%)
    pallas_call x1, Pallas kernels, local(): pl.pallas_call(functools.partial(block_kernel, (n_dp, n_sp, rows, cols, w...  57.2 us
    unnamed x16, local copies, waits for them, and re-layouts  2.33 us
    div x1, other arithmetic, local(): kernel_sum / regions  1.55 us

commit v1 on v0

v1 whole, which is shorter than its diff:
```python
import functools
import math

import jax
import jax.numpy as jnp
from jax import lax
from jax.experimental import pallas as pl
from jax.experimental.pallas import tpu as pltpu
from jax.sharding import PartitionSpec as P

F32, BF16 = jnp.float32, jnp.bfloat16
LANES = 128
EDGE = 8


def gelu_pair(preact):
    cumulative = 0.5 * (1.0 + lax.erf(preact * (1.0 / math.sqrt(2.0))))
    density = jnp.exp(-0.5 * preact * preact) * (1.0 / math.sqrt(2.0 * math.pi))
    return (preact * cumulative, cumulative + preact * density)


def remote(src, dst, send_sem, recv_sem, device):
    return pltpu.make_async_remote_copy(
        src_ref=src,
        dst_ref=dst,
        send_sem=send_sem,
        recv_sem=recv_sem,
        device_id=device,
        device_id_type=pl.DeviceIdType.MESH,
    )


def grid_of(chips):
    across = max(k for k in range(1, chips + 1) if chips % k == 0 and k * k <= chips)
    return chips // across, across


def block_kernel(
    sizes,
    x_hbm, cot_hbm, kern_hbm, gain_hbm, bias_hbm, scale_hbm, wup_hbm, wdown_hbm,
    res_ref, dfeat_ref, gup_ref, gdown_ref, gkern_ref, ggain_ref, gbias_ref, gscale_ref,
    x_ref, cot_ref, kern_ref, gain_ref, bias_ref, scale_ref, wup_ref, wdown_ref,
    xpad, gpad, halo_x, halo_g, conv, scaled_ref, dconv, wout, upg, tok, dmx, hid, dpre,
    part_n, part_m, r1n, r1m, chip_n, chip_m, r2n, r2m, own_n, own_m,
    gpart, gsend, grecv, fsend, frecv, dscale, small, ar1, ar2, ar3,
    in_s, hx_s, hx_r, hg_s, hg_r, w_s, w_r, dm_s, dm_r, tk_s, tk_r,
    an_s, an_r, am_s, am_r, bn_s, bn_r, bm_s, bm_r,
    gz_s, gz_r, fi_s, fi_r, s1_s, s1_r, s2_s, s2_r, s3_s, s3_r,
):
    n_dp, n_sp, rows, cols, width, taps = sizes
    chips, share = n_dp // 2, n_dp // n_sp
    down_n, across_n = grid_of(chips)
    margin = taps // 2
    pixels = rows * cols
    half = pixels // 2
    hidden = wdown_ref.shape[0]
    d, s = lax.axis_index("dp"), lax.axis_index("space")
    chip, core = d // 2, lax.rem(d, 2)
    chip_r, chip_c = chip // across_n, lax.rem(chip, across_n)
    sibling = (chip * 2 + (1 - core), s)
    home = d // share
    place = lax.rem(d, share)
    inside = (home == s).astype(jnp.int32)
    mean_by = 1.0 / n_dp

    pairs = (
        (cot_hbm, cot_ref), (scale_hbm, scale_ref), (x_hbm, x_ref), (wup_hbm, wup_ref),
        (kern_hbm, kern_ref), (gain_hbm, gain_ref), (bias_hbm, bias_ref), (wdown_hbm, wdown_ref),
    )
    loads = [pltpu.make_async_copy(src, dst, in_s.at[i]) for i, (src, dst) in enumerate(pairs)]
    for load in loads:
        load.start()

    def is_self(b):
        return jnp.logical_and(home == s, place == b)

    def dp_peer(off):
        return lax.rem(d + off, n_dp)

    def sp_peer(off):
        return lax.rem(s + off, n_sp)

    barrier = pltpu.get_barrier_semaphore()

    def greet(device):
        pl.semaphore_signal(barrier, inc=1, device_id=device, device_id_type=pl.DeviceIdType.MESH)

    for off in range(1, n_dp):
        greet((dp_peer(off), s))
    for off in range(1, n_sp):
        greet((d, sp_peer(off)))
    for b in range(share):
        @pl.when(jnp.logical_not(is_self(b)))
        def _():
            greet((s * share + b, home))

    for padded in (xpad, gpad):
        padded[...] = jnp.zeros(padded.shape, F32)
    dscale[...] = jnp.zeros(dscale.shape, F32)
    small[...] = jnp.zeros(small.shape, F32)
    loads[0].wait()
    loads[1].wait()
    dmx[0] = (scale_ref[...] * cot_ref[...].astype(F32)).astype(BF16)
    loads[2].wait()
    xpad[margin:margin + rows, EDGE:EDGE + cols] = x_ref[...].astype(F32)
    loads[3].wait()
    for t in range(n_dp):
        wout[t] = wup_ref[:, t * hidden:(t + 1) * hidden]
    upg[d] = wout[d]
    for load in loads[4:]:
        load.wait()
    pl.semaphore_wait(barrier, (n_dp - 1) + (n_sp - 1) + share - inside)

    has_up, has_down = s > 0, s < n_sp - 1

    def halo_copies(source, halo, send, recv):
        down = remote(source.at[pl.ds(rows - margin, margin)], halo.at[0], send.at[0], recv.at[0], (d, jnp.minimum(s + 1, n_sp - 1)))
        up = remote(source.at[pl.ds(0, margin)], halo.at[1], send.at[1], recv.at[1], (d, jnp.maximum(s - 1, 0)))
        return down, up

    def halo_start(copies):
        pl.when(has_down)(copies[0].start)
        pl.when(has_up)(copies[1].start)

    def halo_land(copies, halo, padded):
        @pl.when(has_up)
        def _():
            copies[0].wait_recv()
            padded[0:margin, EDGE:EDGE + cols] = halo[0].astype(F32)

        @pl.when(has_down)
        def _():
            copies[1].wait_recv()
            padded[rows + margin:, EDGE:EDGE + cols] = halo[1].astype(F32)

    def halo_sent(copies):
        pl.when(has_down)(copies[0].wait_send)
        pl.when(has_up)(copies[1].wait_send)

    def chip_at(dr, dc):
        return lax.rem(chip_r + dr, down_n) * across_n + lax.rem(chip_c + dc, across_n)

    def place_of(dr, dc):
        return (dr % down_n) * across_n + dc % across_n

    row_peers = [(0, dc) for dc in range(1, across_n)]
    col_peers = [(dr, 0) for dr in range(1, down_n)]
    diagonals = [(dr, dc) for dr in range(1, down_n) for dc in range(1, across_n)]
    started = []

    class Spread:
        def __init__(self, buf, send, recv):
            self.buf, self.send, self.recv, self.count = buf, send, recv, 0

        def push(self, slot, h, to_slot, device):
            span = pl.ds(h * half, half)
            copy = remote(self.buf.at[slot, span], self.buf.at[to_slot, span], self.send.at[self.count], self.recv.at[2 * to_slot + h], device)
            self.count += 1
            copy.start()
            started.append(copy)

        def own(self, order):
            for dr, dc in row_peers:
                self.push(0, order, 2 * place_of(0, -dc), (chip_at(dr, dc) * 2 + core, s))
            for dr, dc in col_peers:
                self.push(0, 1 - order, 2 * place_of(-dr, 0), (chip_at(dr, dc) * 2 + core, s))

        def own_sibling(self):
            for h in range(2):
                self.push(0, h, 1, sibling)

        def wait(self, slot, h):
            span = pl.ds(h * half, half)
            remote(self.buf.at[slot, span], self.buf.at[slot, span], self.send.at[0], self.recv.at[2 * slot + h], sibling).wait_recv()

        def relay(self, peers, h):
            for dr, dc in peers:
                at = place_of(dr, dc)
                self.wait(2 * at, h)
                if dr == 0 and h == 0:
                    for over, _ in col_peers:
                        self.push(2 * at, h, 2 * place_of(-over, dc), (chip_at(over, 0) * 2 + core, s))
                if dc == 0 and h == 1:
                    for _, over in row_peers:
                        self.push(2 * at, h, 2 * place_of(dr, -over), (chip_at(0, over) * 2 + core, s))
                self.push(2 * at, h, 2 * at + 1, sibling)

        def first(self):
            self.relay(row_peers, 0)
            self.relay(col_peers, 1)

        def second(self):
            self.relay(row_peers, 1)
            self.relay(col_peers, 0)

        def corner(self):
            for h in range(2):
                self.relay(diagonals, h)

        def ready(self, slot):
            for h in range(2):
                self.wait(slot, h)

    hx = halo_copies(x_ref, halo_x, hx_s, hx_r)
    halo_start(hx)
    dm, tk = Spread(dmx, dm_s, dm_r), Spread(tok, tk_s, tk_r)
    w_out = [remote(wout.at[dp_peer(off)], upg.at[d], w_s.at[off], w_r.at[d], (dp_peer(off), s)) for off in range(1, n_dp)]
    w_in = [remote(wout.at[dp_peer(off)], upg.at[dp_peer(off)], w_s.at[off], w_r.at[dp_peer(off)], sibling) for off in range(1, n_dp)]
    dm.own(0)
    for copy in w_out:
        copy.start()
    dm.own_sibling()
    dm.own(1)

    near = [(a, i) for a in range(taps) for i in range(rows) if 0 <= i + a - margin < rows]
    far = [(a, i) for a in range(taps) for i in range(rows) if not 0 <= i + a - margin < rows]

    def convolve(padded, flip, lanes, some, totals):
        totals = dict(totals)
        for b in range(taps):
            first = EDGE - margin + b
            window = {}
            for a, i in some:
                if i + a not in window:
                    window[i + a] = padded[i + a, first:first + cols, lanes]
                at = (taps - 1 - a, taps - 1 - b) if flip else (a, b)
                term = kern_ref[at[0], at[1]:at[1] + 1, lanes] * window[i + a]
                totals[i] = totals[i] + term if i in totals else term
        return totals

    def lanes_of(c):
        return pl.ds(pl.multiple_of(c * LANES, LANES), LANES)

    far_rows = sorted({i for _, i in far})

    @pl.loop(0, width // LANES)
    def _(c):
        lanes = lanes_of(c)
        for i, value in convolve(xpad, False, lanes, near, {}).items():
            conv[i * cols:(i + 1) * cols, lanes] = value

    halo_land(hx, halo_x, xpad)

    @pl.loop(0, width // LANES)
    def _(c):
        lanes = lanes_of(c)
        for i, value in convolve(xpad, False, lanes, far, {i: conv[i * cols:(i + 1) * cols, lanes] for i in far_rows}).items():
            conv[i * cols:(i + 1) * cols, lanes] = value

    center = conv[...]
    center = center - jnp.mean(center, axis=-1, keepdims=True)
    inverse = lax.rsqrt(jnp.mean(center * center, axis=-1, keepdims=True) + 1e-06)
    normal = center * inverse
    scaled_ref[...] = normal
    tok[0] = (normal * gain_ref[...] + bias_ref[...]).astype(BF16)

    tk.own(0)
    tk.own_sibling()
    dm.first()
    tk.own(1)
    for copy in w_in:
        copy.wait_recv()

    def nn(a, b):
        return lax.dot_general(a, b, (((1,), (0,)), ((), ())), preferred_element_type=F32)

    def nt(a, b):
        return lax.dot_general(a, b, (((1,), (1,)), ((), ())), preferred_element_type=F32)

    def tn(a, b):
        return lax.dot_general(a, b, (((0,), (0,)), ((), ())), preferred_element_type=F32)

    def cross(kind, to):
        buf, got, send, recv = kind
        return remote(buf.at[to], got.at[to], send.at[to], recv.at[to], sibling)

    def home_copy(kind, dr, dc):
        buf, got, send, recv = kind
        to, slot = place_of(dr, dc), place_of(-dr, -dc)
        return remote(buf.at[to], got.at[slot], send.at[to], recv.at[slot], (chip_at(dr, dc) * 2 + core, s))

    cross_n, cross_m = (part_n, r1n, an_s, an_r), (part_m, r1m, am_s, am_r)
    home_n, home_m = (chip_n, r2n, bn_s, bn_r), (chip_m, r2m, bm_s, bm_r)

    def products(slot):
        up = upg[...].reshape(width, hidden)
        activation, slope = gelu_pair(nn(tok[slot], up))
        act = activation.astype(BF16)
        grad = (nt(dmx[slot], wdown_ref[...]) * slope).astype(BF16)
        hid[slot] = act
        dpre[slot] = grad
        mixed = nn(act, wdown_ref[...])
        dscale[...] += jnp.sum(dmx[slot].astype(F32) * mixed, axis=0, keepdims=True)
        return nt(grad, up), mixed

    def process(dr, dc):
        at = place_of(dr, dc)
        dm.ready(2 * at + 1)
        tk.ready(2 * at + 1)
        normed, mixed = products(2 * at + 1)
        part_n[at] = normed.astype(BF16)
        cross(cross_n, at).start()
        part_m[at] = mixed.astype(BF16)
        cross(cross_m, at).start()
        normed, mixed = products(2 * at)
        if at:
            cross(cross_n, at).wait_recv()
            chip_n[at] = (normed + r1n[at].astype(F32)).astype(BF16)
            home_copy(home_n, dr, dc).start()
            cross(cross_m, at).wait_recv()
            chip_m[at] = (mixed + r1m[at].astype(F32)).astype(BF16)
        else:
            own_n[...] = normed
            own_m[...] = mixed

    def weight_grads(first, last):
        flat = ((last - first) * pixels,)
        for which, (left, right) in enumerate(((tok, dpre), (dmx, hid))):
            term = tn(left[first:last].reshape(flat + (width,)), right[first:last].reshape(flat + (hidden,)))
            if first:
                gpart[which] += term
            else:
                gpart[which] = term

    process(0, 0)
    tk.first()
    dm.second()
    tk.second()
    for peer in row_peers + col_peers:
        process(*peer)
    dm.corner()
    tk.corner()
    for peer in diagonals:
        process(*peer)
    own_n[...] += r1n_own(cross, cross_n, r1n)
    own_m[...] += r1n_own(cross, cross_m, r1m)
    strip = width // n_sp
    part_rows = strip // share

    def plane_copy(which, off, landing):
        to = sp_peer(off)
        slot = to if landing else s
        return remote(gsend.at[which, to], grecv.at[which, slot], gz_s.at[which, off], gz_r.at[which, slot], (d, to))

    weight_grads(0, n_dp)
    for which in range(2):
        for k in range(n_sp):
            gsend[which, k] = gpart[which, k * strip:(k + 1) * strip].astype(BF16)
        for off in range(1, n_sp):
            plane_copy(which, off, False).start()

    others = row_peers + col_peers + diagonals

    def arrive(got, send, recv, own):
        total = own[...]
        for peer in others:
            at = place_of(*peer)
            remote(got.at[at], got.at[at], send.at[at], recv.at[at], sibling).wait_recv()
            total = total + got[at].astype(F32)
        return total

    d_norm = arrive(r2n, bn_s, bn_r, own_n)
    for peer in others:
        home_copy(home_m, *peer).start()
    normal = scaled_ref[...]
    d_hat = d_norm * gain_ref[...]
    lead = jnp.mean(d_hat, axis=-1, keepdims=True)
    second = jnp.mean(d_hat * normal, axis=-1, keepdims=True)
    dconv[...] = (inverse * (d_hat - lead - normal * second)).astype(BF16).reshape(rows, cols, width)
    hg = halo_copies(dconv, halo_g, hg_s, hg_r)
    halo_start(hg)
    gpad[margin:margin + rows, EDGE:EDGE + cols] = dconv[...].astype(F32)

    per = small.shape[1]
    count = taps * taps

    def put(row, lanes, value):
        small[row // per, row % per:row % per + 1, lanes] = value

    everything = slice(None)
    put(count, everything, jnp.sum(d_norm * normal, axis=0, keepdims=True))
    put(count + 1, everything, jnp.sum(d_norm, axis=0, keepdims=True))
    put(count + 2, everything, dscale[...] / scale_ref[...])

    @pl.loop(0, width // LANES)
    def _(c):
        lanes = lanes_of(c)
        upstream = gpad[margin:margin + rows, EDGE:EDGE + cols, lanes]
        for b in range(taps):
            first = EDGE - margin + b
            window = xpad[:, first:first + cols, lanes]
            for a in range(taps):
                product = jnp.sum(window[a:a + rows] * upstream, axis=0)
                put(a * taps + b, lanes, jnp.sum(product, axis=0, keepdims=True))

    s1_out = [remote(small.at[dp_peer(off)], ar1.at[d], s1_s.at[off], s1_r.at[d], (dp_peer(off), s)) for off in range(1, n_dp)]
    s1_in = [remote(small.at[dp_peer(off)], ar1.at[dp_peer(off)], s1_s.at[off], s1_r.at[dp_peer(off)], sibling) for off in range(1, n_dp)]
    for copy in s1_out:
        copy.start()
    ar1[d] = small[d]

    @pl.loop(0, width // LANES)
    def _(c):
        lanes = lanes_of(c)
        cot = {i: cot_ref[i * cols:(i + 1) * cols, lanes].astype(F32) for i in range(rows)}
        for i, value in convolve(gpad, True, lanes, near, cot).items():
            dfeat_ref[i, :, lanes] = value

    for copy in s1_in:
        copy.wait_recv()
    ar2[s] = jnp.sum(ar1[...], axis=0)
    s2_out = [remote(ar2.at[s], ar2.at[s], s2_s.at[off], s2_r.at[s], (d, sp_peer(off))) for off in range(1, n_sp)]
    s2_in = [remote(ar2.at[s], ar2.at[sp_peer(off)], s2_s.at[off], s2_r.at[sp_peer(off)], (d, sp_peer(off))) for off in range(1, n_sp)]
    for copy in s2_out:
        copy.start()

    halo_land(hg, halo_g, gpad)

    @pl.loop(0, width // LANES)
    def _(c):
        lanes = lanes_of(c)
        for i, value in convolve(gpad, True, lanes, far, {i: dfeat_ref[i, :, lanes] for i in far_rows}).items():
            dfeat_ref[i, :, lanes] = value

    def owner_copy(which, b):
        return remote(fsend.at[which, b], frecv.at[which, place], fi_s.at[which, b], fi_r.at[which, place], (s * share + b, home))

    for which in range(2):
        total = gpart[which, pl.ds(pl.multiple_of(s * strip, strip), strip)]
        for off in range(1, n_sp):
            plane_copy(which, off, True).wait_recv()
            total = total + grecv[which, sp_peer(off)].astype(F32)
        for b in range(share):
            fsend[which, b] = total[b * part_rows:(b + 1) * part_rows].astype(BF16)
            pl.when(jnp.logical_not(is_self(b)))(owner_copy(which, b).start)

            @pl.when(is_self(b))
            def _():
                frecv[which, b] = fsend[which, b]

    for copy in s2_in:
        copy.wait_recv()
    ar3[d] = jnp.sum(ar2[...], axis=0) * mean_by
    s3_out = [remote(ar3.at[d], ar3.at[d], s3_s.at[off], s3_r.at[d], (dp_peer(off), s)) for off in range(1, n_dp)]
    s3_in = [remote(ar3.at[d], ar3.at[dp_peer(off)], s3_s.at[off], s3_r.at[dp_peer(off)], sibling) for off in range(1, n_dp)]
    for copy in s3_out:
        copy.start()

    mixed = arrive(r2m, bm_s, bm_r, own_m)
    res_ref[...] = (x_ref[...].reshape(pixels, width).astype(F32) + scale_ref[...] * mixed).astype(BF16).reshape(rows, cols, width)

    for which, out in enumerate((gup_ref, gdown_ref)):
        for b in range(share):
            landed = remote(fsend.at[which, b], frecv.at[which, b], fi_s.at[which, b], fi_r.at[which, b], sibling)
            pl.when(jnp.logical_not(is_self(b)))(landed.wait_recv)
        for b in range(share):
            out[:, b * hidden:(b + 1) * hidden] = frecv[which, b].astype(F32) * mean_by

    for copy in s3_in:
        copy.wait_recv()

    def take(row):
        return ar3[row // per, row % per:row % per + 1]

    for a in range(taps):
        for b in range(taps):
            gkern_ref[a, b:b + 1] = take(a * taps + b)
    ggain_ref[...] = take(count)
    gbias_ref[...] = take(count + 1)
    gscale_ref[...] = take(count + 2)

    halo_sent(hx)
    halo_sent(hg)
    for group in (started, w_out, s1_out, s2_out, s3_out):
        for copy in group:
            copy.wait_send()
    for which in range(2):
        for off in range(1, n_sp):
            plane_copy(which, off, False).wait_send()
        for b in range(share):
            pl.when(jnp.logical_not(is_self(b)))(owner_copy(which, b).wait_send)

    for at in range(chips):
        cross(cross_n, at).wait_send()
        cross(cross_m, at).wait_send()
    for peer in others:
        home_copy(home_n, *peer).wait_send()
        home_copy(home_m, *peer).wait_send()


def r1n_own(cross, kind, got):
    cross(kind, 0).wait_recv()
    return got[0].astype(F32)


def finish_kernel(*refs):
    n = (len(refs) - 1) // 2
    copies = [pltpu.make_async_copy(refs[i], refs[n + i], refs[-1].at[i]) for i in range(n)]
    for copy in copies:
        copy.start()
    for copy in copies:
        copy.wait()


def finish(arrays):
    return pl.pallas_call(
        finish_kernel,
        out_shape=tuple(jax.ShapeDtypeStruct(a.shape, a.dtype) for a in arrays),
        in_specs=[pl.BlockSpec(memory_space=pltpu.VMEM)] * len(arrays),
        out_specs=(pl.BlockSpec(memory_space=pltpu.HBM),) * len(arrays),
        scratch_shapes=[pltpu.SemaphoreType.DMA((len(arrays),))],
        compiler_params=pltpu.CompilerParams(vmem_limit_bytes=4 << 20),
    )(*arrays)


def local(features, cotangent, dw_kernel, ln_gain, ln_bias, layer_scale, w_up, w_down):
    n_dp, n_sp = lax.axis_size("dp"), lax.axis_size("space")
    _, rows, cols, width = features.shape
    taps = dw_kernel.shape[0]
    margin = taps // 2
    pixels = rows * cols
    hidden = w_down.shape[0]
    chips, share = n_dp // 2, n_dp // n_sp
    strip = width // n_sp
    part_rows = strip // share
    count = taps * taps
    per = -(-(count + 3) // n_dp)
    blocks = (n_dp, w_up.shape[0], hidden)
    padded = (rows + 2 * margin, cols + 2 * EDGE, width)
    dma = lambda k: pltpu.SemaphoreType.DMA((k,))
    vm = pltpu.VMEM
    operands = (
        features[0],
        cotangent[0].reshape(pixels, width),
        dw_kernel,
        ln_gain.reshape(1, width),
        ln_bias.reshape(1, width),
        layer_scale.reshape(1, width),
        w_up,
        w_down,
    )
    operands = tuple(pltpu.with_memory_space_constraint(a, pltpu.HBM) for a in operands)
    scratch = [vm(a.shape, a.dtype) for a in operands]
    scratch += [
        vm(padded, F32), vm(padded, F32),
        vm((2, margin, cols, width), BF16), vm((2, margin, cols, width), BF16),
        vm((pixels, width), F32), vm((pixels, width), F32), vm((rows, cols, width), BF16),
        vm(blocks, BF16), vm(blocks, BF16),
        vm((n_dp, pixels, width), BF16), vm((n_dp, pixels, width), BF16),
        vm((n_dp, pixels, hidden), BF16), vm((n_dp, pixels, hidden), BF16),
    ]
    scratch += [vm((chips, pixels, width), BF16)] * 8
    scratch += [vm((pixels, width), F32)] * 2
    scratch += [
        vm((2, width, hidden), F32),
        vm((2, n_sp, strip, hidden), BF16), vm((2, n_sp, strip, hidden), BF16),
        vm((2, share, part_rows, hidden), BF16), vm((2, share, part_rows, hidden), BF16),
        vm((1, width), F32),
        vm((n_dp, per, width), F32), vm((n_dp, per, width), F32),
        vm((n_sp, per, width), F32), vm((n_dp, per, width), F32),
    ]
    scratch += [dma(len(operands))] + [dma(2)] * 4 + [dma(n_dp)] * 2 + [dma(2 * n_dp)] * 4 + [dma(chips)] * 8
    pair = lambda k: pltpu.SemaphoreType.DMA((2, k))
    scratch += [pair(n_sp)] * 2 + [pair(share)] * 2 + [dma(n_dp)] * 2 + [dma(n_sp)] * 2 + [dma(n_dp)] * 2
    outputs = pl.pallas_call(
        functools.partial(block_kernel, (n_dp, n_sp, rows, cols, width, taps)),
        out_shape=(
            vm((rows, cols, width), BF16),
            vm((rows, cols, width), F32),
            vm((part_rows, share * hidden), F32),
            vm((part_rows, share * hidden), F32),
            vm((taps, taps, width), F32),
        )
        + (vm((1, width), F32),) * 3,
        in_specs=[pl.BlockSpec(memory_space=pltpu.HBM)] * 8,
        out_specs=(pl.BlockSpec(memory_space=pltpu.VMEM),) * 8,
        scratch_shapes=scratch,
        compiler_params=pltpu.CompilerParams(
            collective_id=0, has_side_effects=True, vmem_limit_bytes=40 << 20
        ),
    )(*operands)
    result, d_feat, grad_up, grad_down, kernel_sum, gain_sum, bias_sum, scale_sum = finish(outputs)
    return (
        result[None],
        d_feat[None],
        grad_up,
        grad_down.T,
        kernel_sum,
        gain_sum[0],
        bias_sum[0],
        scale_sum[0],
    )


def solution(mesh):
    in_specs = (
        P("dp", "space", None, None),
        P("dp", "space", None, None),
        P(),
        P(),
        P(),
        P(),
        P("dp", None),
        P("dp", None),
    )
    out_specs = (
        P("dp", "space", None, None),
        P("dp", "space", None, None),
        P("dp", "space"),
        P("space", "dp"),
        P(),
        P(),
        P(),
        P(),
    )
    return jax.shard_map(local, mesh=mesh, in_specs=in_specs, out_specs=out_specs, check_vma=False)
```

time: 63.8 us -> 53.4 us (0.84)
  Pallas kernels: 57.2 us -> 52.7 us
  other arithmetic: 3.44 us -> 0 us
  local copies, waits for them, and re-layouts: 2.33 us -> 0 us
    pallas_call x1, Pallas kernels: 57.2 us -> 51.7 us  [local(): pl.pallas_call(functools.partial(block_kernel, (n_dp, n_sp, rows, cols, w...]
    div x4 -> x0, other arithmetic: 3.44 us -> none  [the longest x1 1.55 us: local(): kernel_sum / regions]
    unnamed x16 -> x0, local copies, waits for them, and re-layouts: 2.33 us -> none
    pallas_call x0 -> x1, Pallas kernels: none -> 0.94 us  [finish(): pl.pallas_call(finish_kernel, out_shape=tuple((jax.ShapeDtypeStruct(a.sha...]
where the time goes in v1:
time: 53.4 us; the launch traced here: 53.3 us
  Pallas kernels  52.7 us (99%)
  between operations  0.64 us (1%)
    pallas_call x1, Pallas kernels, local(): pl.pallas_call(functools.partial(block_kernel, (n_dp, n_sp, rows, cols, w...  51.7 us

profile of v1, /device:TPU:3, one launch (start us, length us, event | category | flops | bytes accessed | tf_op | source)
XLA Modules:
  0.0 53.3 jit_solution(4054582771347911980)
XLA Ops:
  0.6 51.7 %shard_map.143 = (bf16[8,16,512]{2,1,0:T(8,128)(2,1)S(1)}, f32[8,16,512]{2,1,0:T(8,128)S(1)}, f32[64,512]{1,0:T(8,128)S(1)}, f32[64,512]{1,0:T(8,128)S(1)}, f32[...) custom-call(bf16[8,16,512]{2,1,0:T(8,128)(2,1)} %bitcast.11, ...), custom_call_target="tpu_custom_call" | custom-call | tf_op jit(solution)/shard_map/pallas_call | solution.py:565
  52.4 0.9 %shard_map.144 = (bf16[8,16,512]{2,1,0:T(8,128)(2,1)}, f32[8,16,512]{2,1,0:T(8,128)}, f32[64,512]{1,0:T(8,128)}, f32[64,512]{1,0:T(8,128)}, f32[7,7,512]{2,1,0:T...) custom-call(bf16[8,16,512]{2,1,0:T(8,128)(2,1)S(1)} %get-tuple-element.24.refs_0_, ...), custom_call_target="tpu_custom_call" | custom-call | tf_op jit(solution)/shard_map/pallas_call | solution.py:506

commit v2 on v1

--- a/solution.py
+++ b/solution.py
@@ -39,13 +39,13 @@
     sizes,
     x_hbm, cot_hbm, kern_hbm, gain_hbm, bias_hbm, scale_hbm, wup_hbm, wdown_hbm,
     res_ref, dfeat_ref, gup_ref, gdown_ref, gkern_ref, ggain_ref, gbias_ref, gscale_ref,
-    x_ref, cot_ref, kern_ref, gain_ref, bias_ref, scale_ref, wup_ref, wdown_ref,
-    xpad, gpad, halo_x, halo_g, conv, scaled_ref, dconv, wout, upg, tok, dmx, hid, dpre,
-    part_n, part_m, r1n, r1m, chip_n, chip_m, r2n, r2m, own_n, own_m,
-    gpart, gsend, grecv, fsend, frecv, dscale, small, ar1, ar2, ar3,
-    in_s, hx_s, hx_r, hg_s, hg_r, w_s, w_r, dm_s, dm_r, tk_s, tk_r,
-    an_s, an_r, am_s, am_r, bn_s, bn_r, bm_s, bm_r,
-    gz_s, gz_r, fi_s, fi_r, s1_s, s1_r, s2_s, s2_r, s3_s, s3_r,
+    x_ref, cot_ref, kern_ref, gain_ref, bias_ref, scale_ref, wup_ref,
+    xpad, gpad, halo_x, halo_g, conv, scaled_ref, dconv, wout, upg, wdn, tok, dmx, hid, dpre,
+    chip_n, chip_m, r2n, r2m, own_n, own_m,
+    gpart, gswap, gback, gsend, grecv, gown, fsend, frecv, dscale, small, ar1, ar2, ar3,
+    in_s, hx_s, hx_r, hg_s, hg_r, w_s, w_r, wd_s, wd_r, dm_s, dm_r, tk_s, tk_r,
+    bn_s, bn_r, bm_s, bm_r,
+    gx_s, gx_r, gz_s, gz_r, fi_s, fi_r, s1_s, s1_r, s2_s, s2_r, s3_s, s3_r,
 ):
     n_dp, n_sp, rows, cols, width, taps = sizes
     chips, share = n_dp // 2, n_dp // n_sp
@@ -53,7 +53,7 @@
     margin = taps // 2
     pixels = rows * cols
     half = pixels // 2
-    hidden = wdown_ref.shape[0]
+    hidden = wdown_hbm.shape[0]
     d, s = lax.axis_index("dp"), lax.axis_index("space")
     chip, core = d // 2, lax.rem(d, 2)
     chip_r, chip_c = chip // across_n, lax.rem(chip, across_n)
@@ -65,7 +65,7 @@
 
     pairs = (
         (cot_hbm, cot_ref), (scale_hbm, scale_ref), (x_hbm, x_ref), (wup_hbm, wup_ref),
-        (kern_hbm, kern_ref), (gain_hbm, gain_ref), (bias_hbm, bias_ref), (wdown_hbm, wdown_ref),
+        (kern_hbm, kern_ref), (gain_hbm, gain_ref), (bias_hbm, bias_ref), (wdown_hbm, wdn.at[core]),
     )
     loads = [pltpu.make_async_copy(src, dst, in_s.at[i]) for i, (src, dst) in enumerate(pairs)]
     for load in loads:
@@ -105,8 +105,8 @@
     xpad[margin:margin + rows, EDGE:EDGE + cols] = x_ref[...].astype(F32)
     loads[3].wait()
     for t in range(n_dp):
-        wout[t] = wup_ref[:, t * hidden:(t + 1) * hidden]
-    upg[d] = wout[d]
+        wout[t // 2, t % 2] = wup_ref[:, t * hidden:(t + 1) * hidden]
+    upg[d] = wout[chip]
     for load in loads[4:]:
         load.wait()
     pl.semaphore_wait(barrier, (n_dp - 1) + (n_sp - 1) + share - inside)
@@ -152,64 +152,62 @@
         def __init__(self, buf, send, recv):
             self.buf, self.send, self.recv, self.count = buf, send, recv, 0
 
-        def push(self, slot, h, to_slot, device):
+        def push(self, slot, h, to_slot, dr, dc):
             span = pl.ds(h * half, half)
-            copy = remote(self.buf.at[slot, span], self.buf.at[to_slot, span], self.send.at[self.count], self.recv.at[2 * to_slot + h], device)
+            copy = remote(self.buf.at[slot, span], self.buf.at[to_slot, span], self.send.at[self.count], self.recv.at[2 * to_slot + h], (chip_at(dr, dc) * 2 + core, s))
             self.count += 1
             copy.start()
             started.append(copy)
 
         def own(self, order):
             for dr, dc in row_peers:
-                self.push(0, order, 2 * place_of(0, -dc), (chip_at(dr, dc) * 2 + core, s))
+                self.push(0, order, place_of(0, -dc), dr, dc)
             for dr, dc in col_peers:
-                self.push(0, 1 - order, 2 * place_of(-dr, 0), (chip_at(dr, dc) * 2 + core, s))
-
-        def own_sibling(self):
-            for h in range(2):
-                self.push(0, h, 1, sibling)
+                self.push(0, 1 - order, place_of(-dr, 0), dr, dc)
 
         def wait(self, slot, h):
             span = pl.ds(h * half, half)
             remote(self.buf.at[slot, span], self.buf.at[slot, span], self.send.at[0], self.recv.at[2 * slot + h], sibling).wait_recv()
 
-        def relay(self, peers, h):
-            for dr, dc in peers:
-                at = place_of(dr, dc)
-                self.wait(2 * at, h)
-                if dr == 0 and h == 0:
-                    for over, _ in col_peers:
-                        self.push(2 * at, h, 2 * place_of(-over, dc), (chip_at(over, 0) * 2 + core, s))
-                if dc == 0 and h == 1:
-                    for _, over in row_peers:
-                        self.push(2 * at, h, 2 * place_of(dr, -over), (chip_at(0, over) * 2 + core, s))
-                self.push(2 * at, h, 2 * at + 1, sibling)
-
         def first(self):
-            self.relay(row_peers, 0)
-            self.relay(col_peers, 1)
-
-        def second(self):
-            self.relay(row_peers, 1)
-            self.relay(col_peers, 0)
-
-        def corner(self):
+            for dr, dc in row_peers:
+                self.wait(place_of(dr, dc), 0)
+                for over, _ in col_peers:
+                    self.push(place_of(dr, dc), 0, place_of(-over, dc), over, 0)
+            for dr, dc in col_peers:
+                self.wait(place_of(dr, dc), 1)
+                for _, over in row_peers:
+                    self.push(place_of(dr, dc), 1, place_of(dr, -over), 0, over)
+
+        def second(self, dr, dc):
+            self.wait(place_of(dr, dc), 1 if dr == 0 else 0)
+
+        def corner(self, dr, dc):
             for h in range(2):
-                self.relay(diagonals, h)
-
-        def ready(self, slot):
-            for h in range(2):
-                self.wait(slot, h)
+                self.wait(place_of(dr, dc), h)
 
     hx = halo_copies(x_ref, halo_x, hx_s, hx_r)
     halo_start(hx)
     dm, tk = Spread(dmx, dm_s, dm_r), Spread(tok, tk_s, tk_r)
-    w_out = [remote(wout.at[dp_peer(off)], upg.at[d], w_s.at[off], w_r.at[d], (dp_peer(off), s)) for off in range(1, n_dp)]
-    w_in = [remote(wout.at[dp_peer(off)], upg.at[dp_peer(off)], w_s.at[off], w_r.at[dp_peer(off)], sibling) for off in range(1, n_dp)]
+    wd_out = remote(wdn.at[core], wdn.at[core], wd_s.at[0], wd_r.at[0], sibling)
+    wd_in = remote(wdn.at[1 - core], wdn.at[1 - core], wd_s.at[0], wd_r.at[0], sibling)
+
+    def w_pass(source, index):
+        copy = remote(upg.at[source], upg.at[source], w_s.at[index], w_r.at[source], sibling)
+        copy.start()
+        started.append(copy)
+
+    def w_land(source):
+        remote(upg.at[source], upg.at[source], w_s.at[0], w_r.at[source], sibling).wait_recv()
+
+    for i, off in enumerate(range(1, chips)):
+        other = lax.rem(chip + off, chips)
+        copy = remote(wout.at[other], upg.at[d], w_s.at[i], w_r.at[d], (other * 2 + core, s))
+        copy.start()
+        started.append(copy)
+    wd_out.start()
+    w_pass(d, chips - 1)
     dm.own(0)
-    for copy in w_out:
-        copy.start()
-    dm.own_sibling()
     dm.own(1)
 
     near = [(a, i) for a in range(taps) for i in range(rows) if 0 <= i + a - margin < rows]
@@ -255,11 +253,15 @@
     tok[0] = (normal * gain_ref[...] + bias_ref[...]).astype(BF16)
 
     tk.own(0)
-    tk.own_sibling()
+    tk.own(1)
+    for off in range(1, chips):
+        source = lax.rem(chip + off, chips) * 2 + core
+        w_land(source)
+        w_pass(source, chips - 1 + off)
     dm.first()
-    tk.own(1)
-    for copy in w_in:
-        copy.wait_recv()
+    wd_in.wait_recv()
+    for off in range(chips):
+        w_land(lax.rem(chip + off, chips) * 2 + 1 - core)
 
     def nn(a, b):
         return lax.dot_general(a, b, (((1,), (0,)), ((), ())), preferred_element_type=F32)
@@ -269,71 +271,46 @@
 
     def tn(a, b):
         return lax.dot_general(a, b, (((0,), (0,)), ((), ())), preferred_element_type=F32)
-
-    def cross(kind, to):
-        buf, got, send, recv = kind
-        return remote(buf.at[to], got.at[to], send.at[to], recv.at[to], sibling)
 
     def home_copy(kind, dr, dc):
         buf, got, send, recv = kind
         to, slot = place_of(dr, dc), place_of(-dr, -dc)
         return remote(buf.at[to], got.at[slot], send.at[to], recv.at[slot], (chip_at(dr, dc) * 2 + core, s))
 
-    cross_n, cross_m = (part_n, r1n, an_s, an_r), (part_m, r1m, am_s, am_r)
     home_n, home_m = (chip_n, r2n, bn_s, bn_r), (chip_m, r2m, bm_s, bm_r)
-
-    def products(slot):
-        up = upg[...].reshape(width, hidden)
-        activation, slope = gelu_pair(nn(tok[slot], up))
-        act = activation.astype(BF16)
-        grad = (nt(dmx[slot], wdown_ref[...]) * slope).astype(BF16)
-        hid[slot] = act
-        dpre[slot] = grad
-        mixed = nn(act, wdown_ref[...])
-        dscale[...] += jnp.sum(dmx[slot].astype(F32) * mixed, axis=0, keepdims=True)
-        return nt(grad, up), mixed
 
     def process(dr, dc):
         at = place_of(dr, dc)
-        dm.ready(2 * at + 1)
-        tk.ready(2 * at + 1)
-        normed, mixed = products(2 * at + 1)
-        part_n[at] = normed.astype(BF16)
-        cross(cross_n, at).start()
-        part_m[at] = mixed.astype(BF16)
-        cross(cross_m, at).start()
-        normed, mixed = products(2 * at)
+        mixed, normed = None, None
+        for j in range(2):
+            up = upg[:, j].reshape(width, hidden)
+            activation, slope = gelu_pair(nn(tok[at], up))
+            act = activation.astype(BF16)
+            grad = (nt(dmx[at], wdn[j]) * slope).astype(BF16)
+            hid[j, at] = act
+            dpre[j, at] = grad
+            normed_j, mixed_j = nt(grad, up), nn(act, wdn[j])
+            normed = normed_j if normed is None else normed + normed_j
+            mixed = mixed_j if mixed is None else mixed + mixed_j
         if at:
-            cross(cross_n, at).wait_recv()
-            chip_n[at] = (normed + r1n[at].astype(F32)).astype(BF16)
+            chip_n[at] = normed.astype(BF16)
             home_copy(home_n, dr, dc).start()
-            cross(cross_m, at).wait_recv()
-            chip_m[at] = (mixed + r1m[at].astype(F32)).astype(BF16)
+            chip_m[at] = mixed.astype(BF16)
         else:
             own_n[...] = normed
             own_m[...] = mixed
-
-    def weight_grads(first, last):
-        flat = ((last - first) * pixels,)
-        for which, (left, right) in enumerate(((tok, dpre), (dmx, hid))):
-            term = tn(left[first:last].reshape(flat + (width,)), right[first:last].reshape(flat + (hidden,)))
-            if first:
-                gpart[which] += term
-            else:
-                gpart[which] = term
+        dscale[...] += jnp.sum(dmx[at].astype(F32) * mixed, axis=0, keepdims=True)
 
     process(0, 0)
     tk.first()
-    dm.second()
-    tk.second()
     for peer in row_peers + col_peers:
+        dm.second(*peer)
+        tk.second(*peer)
         process(*peer)
-    dm.corner()
-    tk.corner()
     for peer in diagonals:
+        dm.corner(*peer)
+        tk.corner(*peer)
         process(*peer)
-    own_n[...] += r1n_own(cross, cross_n, r1n)
-    own_m[...] += r1n_own(cross, cross_m, r1m)
     strip = width // n_sp
     part_rows = strip // share
 
@@ -342,12 +319,28 @@
         slot = to if landing else s
         return remote(gsend.at[which, to], grecv.at[which, slot], gz_s.at[which, off], gz_r.at[which, slot], (d, to))
 
-    weight_grads(0, n_dp)
+    def swap_copy(which, k):
+        return remote(gswap.at[which, k], gback.at[which, k], gx_s.at[which, k], gx_r.at[which, k], sibling)
+
+    flat = (chips * pixels,)
+    for which, (left, right) in enumerate(((tok, dpre), (dmx, hid))):
+        tall = left[...].reshape(flat + (width,))
+        for j in range(2):
+            gpart[which, j] = tn(tall, right[j].reshape(flat + (hidden,)))
+        for off in [*range(1, n_sp), 0]:
+            k = sp_peer(off)
+            gswap[which, k] = gpart[which, 1 - core, pl.ds(pl.multiple_of(k * strip, strip), strip)].astype(BF16)
+            swap_copy(which, k).start()
     for which in range(2):
-        for k in range(n_sp):
-            gsend[which, k] = gpart[which, k * strip:(k + 1) * strip].astype(BF16)
-        for off in range(1, n_sp):
-            plane_copy(which, off, False).start()
+        for off in [*range(1, n_sp), 0]:
+            k = sp_peer(off)
+            swap_copy(which, k).wait_recv()
+            total = gpart[which, core, pl.ds(pl.multiple_of(k * strip, strip), strip)] + gback[which, k].astype(F32)
+            if off:
+                gsend[which, k] = total.astype(BF16)
+                plane_copy(which, off, False).start()
+            else:
+                gown[which] = total
 
     others = row_peers + col_peers + diagonals
 
@@ -360,7 +353,7 @@
         return total
 
     d_norm = arrive(r2n, bn_s, bn_r, own_n)
-    for peer in others:
+    for peer in row_peers + col_peers:
         home_copy(home_m, *peer).start()
     normal = scaled_ref[...]
     d_hat = d_norm * gain_ref[...]
@@ -397,6 +390,8 @@
     s1_in = [remote(small.at[dp_peer(off)], ar1.at[dp_peer(off)], s1_s.at[off], s1_r.at[dp_peer(off)], sibling) for off in range(1, n_dp)]
     for copy in s1_out:
         copy.start()
+    for peer in diagonals:
+        home_copy(home_m, *peer).start()
     ar1[d] = small[d]
 
     @pl.loop(0, width // LANES)
@@ -426,7 +421,7 @@
         return remote(fsend.at[which, b], frecv.at[which, place], fi_s.at[which, b], fi_r.at[which, place], (s * share + b, home))
 
     for which in range(2):
-        total = gpart[which, pl.ds(pl.multiple_of(s * strip, strip), strip)]
+        total = gown[which]
         for off in range(1, n_sp):
             plane_copy(which, off, True).wait_recv()
             total = total + grecv[which, sp_peer(off)].astype(F32)
@@ -471,7 +466,8 @@
 
     halo_sent(hx)
     halo_sent(hg)
-    for group in (started, w_out, s1_out, s2_out, s3_out):
+    wd_out.wait_send()
+    for group in (started, s1_out, s2_out, s3_out):
         for copy in group:
             copy.wait_send()
     for which in range(2):
@@ -480,17 +476,12 @@
         for b in range(share):
             pl.when(jnp.logical_not(is_self(b)))(owner_copy(which, b).wait_send)
 
-    for at in range(chips):
-        cross(cross_n, at).wait_send()
-        cross(cross_m, at).wait_send()
+    for which in range(2):
+        for k in range(n_sp):
+            swap_copy(which, k).wait_send()
     for peer in others:
         home_copy(home_n, *peer).wait_send()
         home_copy(home_m, *peer).wait_send()
-
-
-def r1n_own(cross, kind, got):
-    cross(kind, 0).wait_recv()
-    return got[0].astype(F32)
 
 
 def finish_kernel(*refs):
@@ -525,7 +516,7 @@
     part_rows = strip // share
     count = taps * taps
     per = -(-(count + 3) // n_dp)
-    blocks = (n_dp, w_up.shape[0], hidden)
+    block = (2, w_up.shape[0], hidden)
     padded = (rows + 2 * margin, cols + 2 * EDGE, width)
     dma = lambda k: pltpu.SemaphoreType.DMA((k,))
     vm = pltpu.VMEM
@@ -540,28 +531,31 @@
         w_down,
     )
     operands = tuple(pltpu.with_memory_space_constraint(a, pltpu.HBM) for a in operands)
-    scratch = [vm(a.shape, a.dtype) for a in operands]
+    scratch = [vm(a.shape, a.dtype) for a in operands[:-1]]
     scratch += [
         vm(padded, F32), vm(padded, F32),
         vm((2, margin, cols, width), BF16), vm((2, margin, cols, width), BF16),
         vm((pixels, width), F32), vm((pixels, width), F32), vm((rows, cols, width), BF16),
-        vm(blocks, BF16), vm(blocks, BF16),
-        vm((n_dp, pixels, width), BF16), vm((n_dp, pixels, width), BF16),
-        vm((n_dp, pixels, hidden), BF16), vm((n_dp, pixels, hidden), BF16),
+        vm((chips,) + block, BF16), vm((n_dp,) + block, BF16), vm((2, hidden, width), BF16),
+        vm((chips, pixels, width), BF16), vm((chips, pixels, width), BF16),
+        vm((2, chips, pixels, hidden), BF16), vm((2, chips, pixels, hidden), BF16),
     ]
-    scratch += [vm((chips, pixels, width), BF16)] * 8
+    scratch += [vm((chips, pixels, width), BF16)] * 4
     scratch += [vm((pixels, width), F32)] * 2
     scratch += [
-        vm((2, width, hidden), F32),
-        vm((2, n_sp, strip, hidden), BF16), vm((2, n_sp, strip, hidden), BF16),
+        vm((2, 2, width, hidden), F32),
+    ]
+    scratch += [vm((2, n_sp, strip, hidden), BF16)] * 4
+    scratch += [
+        vm((2, strip, hidden), F32),
         vm((2, share, part_rows, hidden), BF16), vm((2, share, part_rows, hidden), BF16),
         vm((1, width), F32),
         vm((n_dp, per, width), F32), vm((n_dp, per, width), F32),
         vm((n_sp, per, width), F32), vm((n_dp, per, width), F32),
     ]
-    scratch += [dma(len(operands))] + [dma(2)] * 4 + [dma(n_dp)] * 2 + [dma(2 * n_dp)] * 4 + [dma(chips)] * 8
+    scratch += [dma(len(operands))] + [dma(2)] * 4 + [dma(n_dp)] * 2 + [dma(1)] * 2 + [dma(n_dp)] * 4 + [dma(chips)] * 4
     pair = lambda k: pltpu.SemaphoreType.DMA((2, k))
-    scratch += [pair(n_sp)] * 2 + [pair(share)] * 2 + [dma(n_dp)] * 2 + [dma(n_sp)] * 2 + [dma(n_dp)] * 2
+    scratch += [pair(n_sp)] * 4 + [pair(share)] * 2 + [dma(n_dp)] * 2 + [dma(n_sp)] * 2 + [dma(n_dp)] * 2
     outputs = pl.pallas_call(
         functools.partial(block_kernel, (n_dp, n_sp, rows, cols, width, taps)),
         out_shape=(

time: 53.4 us -> 47.5 us (0.89)
  Pallas kernels: 52.7 us -> 46.7 us
    pallas_call x1, Pallas kernels: 51.7 us -> 45.8 us  [local(): pl.pallas_call(functools.partial(block_kernel, (n_dp, n_sp, rows, cols, w...]
where the time goes in v2:
time: 47.5 us; the launch traced here: 47.4 us
  Pallas kernels  46.7 us (98%)
  between operations  0.64 us (1%)
    pallas_call x1, Pallas kernels, local(): pl.pallas_call(functools.partial(block_kernel, (n_dp, n_sp, rows, cols, w...  45.8 us

profile of v2, /device:TPU:3, one launch (start us, length us, event | category | flops | bytes accessed | tf_op | source)
XLA Modules:
  0.0 47.4 jit_solution(10407111646681615381)
XLA Ops:
  0.6 45.8 %shard_map.143 = (bf16[8,16,512]{2,1,0:T(8,128)(2,1)S(1)}, f32[8,16,512]{2,1,0:T(8,128)S(1)}, f32[64,512]{1,0:T(8,128)S(1)}, f32[64,512]{1,0:T(8,128)S(1)}, f32[...) custom-call(bf16[8,16,512]{2,1,0:T(8,128)(2,1)} %bitcast.11, ...), custom_call_target="tpu_custom_call" | custom-call | tf_op jit(solution)/shard_map/pallas_call | solution.py:559
  46.4 0.9 %shard_map.144 = (bf16[8,16,512]{2,1,0:T(8,128)(2,1)}, f32[8,16,512]{2,1,0:T(8,128)}, f32[64,512]{1,0:T(8,128)}, f32[64,512]{1,0:T(8,128)}, f32[7,7,512]{2,1,0:T...) custom-call(bf16[8,16,512]{2,1,0:T(8,128)(2,1)S(1)} %get-tuple-element.24.refs_0_, ...), custom_call_target="tpu_custom_call" | custom-call | tf_op jit(solution)/shard_map/pallas_call | solution.py:497

commit v3 on v2

--- a/solution.py
+++ b/solution.py
@@ -42,10 +42,10 @@
     x_ref, cot_ref, kern_ref, gain_ref, bias_ref, scale_ref, wup_ref,
     xpad, gpad, halo_x, halo_g, conv, scaled_ref, dconv, wout, upg, wdn, tok, dmx, hid, dpre,
     chip_n, chip_m, r2n, r2m, own_n, own_m,
-    gpart, gswap, gback, gsend, grecv, gown, fsend, frecv, dscale, small, ar1, ar2, ar3,
+    gpart, gswap, gback, gsend, grecv, gown, ghold, gpass, fsend, frecv, dscale, small, ar1, ar2, ar3,
     in_s, hx_s, hx_r, hg_s, hg_r, w_s, w_r, wd_s, wd_r, dm_s, dm_r, tk_s, tk_r,
     bn_s, bn_r, bm_s, bm_r,
-    gx_s, gx_r, gz_s, gz_r, fi_s, fi_r, s1_s, s1_r, s2_s, s2_r, s3_s, s3_r,
+    gx_s, gx_r, gz_s, gz_r, gp_r, fi_s, fi_r, s1_s, s1_r, s2_s, s2_r, s3_s, s3_r,
 ):
     n_dp, n_sp, rows, cols, width, taps = sizes
     chips, share = n_dp // 2, n_dp // n_sp
@@ -98,6 +98,10 @@
         padded[...] = jnp.zeros(padded.shape, F32)
     dscale[...] = jnp.zeros(dscale.shape, F32)
     small[...] = jnp.zeros(small.shape, F32)
+    for edge, unused in ((0, n_sp - 1), (n_sp - 1, 0)):
+        @pl.when(s == edge)
+        def _():
+            grecv[:, unused] = jnp.zeros((2,) + grecv.shape[2:], BF16)
     loads[0].wait()
     loads[1].wait()
     dmx[0] = (scale_ref[...] * cot_ref[...].astype(F32)).astype(BF16)
@@ -277,7 +281,19 @@
         to, slot = place_of(dr, dc), place_of(-dr, -dc)
         return remote(buf.at[to], got.at[slot], send.at[to], recv.at[slot], (chip_at(dr, dc) * 2 + core, s))
 
-    home_n, home_m = (chip_n, r2n, bn_s, bn_r), (chip_m, r2m, bm_s, bm_r)
+    home_n = (chip_n, r2n, bn_s, bn_r)
+
+    def home_half(dr, dc, h):
+        to, slot, span = place_of(dr, dc), place_of(-dr, -dc), pl.ds(h * half, half)
+        return remote(chip_m.at[to, span], r2m.at[slot, span], bm_s.at[2 * to + h], bm_r.at[2 * slot + h], (chip_at(dr, dc) * 2 + core, s))
+
+    def weight_grads(which, first, last):
+        left, right = ((tok, dpre), (dmx, hid))[which]
+        flat = ((last - first) * pixels,)
+        tall = left[first:last].reshape(flat + (width,))
+        for j in range(2):
+            term = tn(tall, right[j, first:last].reshape(flat + (hidden,)))
+            gpart[which, j] = gpart[which, j] + term if first else term
 
     def process(dr, dc):
         at = place_of(dr, dc)
@@ -307,6 +323,10 @@
         dm.second(*peer)
         tk.second(*peer)
         process(*peer)
+    done = {0} | {place_of(*peer) for peer in row_peers + col_peers}
+    lead = next(at for at in range(chips + 1) if at not in done)
+    for which in range(2):
+        weight_grads(which, 0, lead)
     for peer in diagonals:
         dm.corner(*peer)
         tk.corner(*peer)
@@ -314,47 +334,77 @@
     strip = width // n_sp
     part_rows = strip // share
 
-    def plane_copy(which, off, landing):
-        to = sp_peer(off)
-        slot = to if landing else s
-        return remote(gsend.at[which, to], grecv.at[which, slot], gz_s.at[which, off], gz_r.at[which, slot], (d, to))
+    bend = n_sp >= 4
+    relay_dev = jnp.logical_or(s == 1, s == n_sp - 2)
+    far_of_relay = jnp.where(s == 1, n_sp - 1, 0)
+    near_edge = jnp.where(s == 0, 1, n_sp - 2)
+
+    def far_pair(k):
+        return jnp.logical_and(bend, abs(s - k) == n_sp - 1)
+
+    def relays(k):
+        return jnp.logical_and(jnp.logical_and(bend, relay_dev), k == far_of_relay)
+
+    def plane_copy(which, k):
+        return remote(gsend.at[which, k], grecv.at[which, s], gz_s.at[which, k], gz_r.at[which, s], (d, k))
+
+    def bent_copy(which, k):
+        return remote(gsend.at[which, k], gpass.at[which], gz_s.at[which, k], gp_r.at[which], (d, near_edge))
+
+    def plane_land(which, k):
+        remote(gsend.at[which, k], grecv.at[which, k], gz_s.at[which, k], gz_r.at[which, k], (d, k)).wait_recv()
+
+    def toward(i):
+        return lax.rem(s + jnp.where(2 * s < n_sp, n_sp - i, i), n_sp)
 
     def swap_copy(which, k):
         return remote(gswap.at[which, k], gback.at[which, k], gx_s.at[which, k], gx_r.at[which, k], sibling)
 
-    flat = (chips * pixels,)
-    for which, (left, right) in enumerate(((tok, dpre), (dmx, hid))):
-        tall = left[...].reshape(flat + (width,))
-        for j in range(2):
-            gpart[which, j] = tn(tall, right[j].reshape(flat + (hidden,)))
-        for off in [*range(1, n_sp), 0]:
-            k = sp_peer(off)
+    for which in range(2):
+        if lead < chips:
+            weight_grads(which, lead, chips)
+        for i in [*range(1, n_sp), 0]:
+            k = toward(i)
             gswap[which, k] = gpart[which, 1 - core, pl.ds(pl.multiple_of(k * strip, strip), strip)].astype(BF16)
             swap_copy(which, k).start()
     for which in range(2):
-        for off in [*range(1, n_sp), 0]:
-            k = sp_peer(off)
+        for i in [*range(1, n_sp), 0]:
+            k = toward(i)
             swap_copy(which, k).wait_recv()
             total = gpart[which, core, pl.ds(pl.multiple_of(k * strip, strip), strip)] + gback[which, k].astype(F32)
-            if off:
-                gsend[which, k] = total.astype(BF16)
-                plane_copy(which, off, False).start()
-            else:
+            if not i:
                 gown[which] = total
+                continue
+            gsend[which, k] = total.astype(BF16)
+
+            @pl.when(relays(k))
+            def _():
+                ghold[which] = total
+
+            @pl.when(far_pair(k))
+            def _():
+                bent_copy(which, k).start()
+
+            @pl.when(jnp.logical_not(jnp.logical_or(far_pair(k), relays(k))))
+            def _():
+                plane_copy(which, k).start()
+    def relay(which):
+        if bend:
+            @pl.when(relay_dev)
+            def _():
+                remote(gsend.at[which, s], gpass.at[which], gz_s.at[which, s], gp_r.at[which], sibling).wait_recv()
+                gsend[which, far_of_relay] = (ghold[which] + gpass[which].astype(F32)).astype(BF16)
+                plane_copy(which, far_of_relay).start()
 
     others = row_peers + col_peers + diagonals
 
-    def arrive(got, send, recv, own):
-        total = own[...]
-        for peer in others:
-            at = place_of(*peer)
-            remote(got.at[at], got.at[at], send.at[at], recv.at[at], sibling).wait_recv()
-            total = total + got[at].astype(F32)
-        return total
-
-    d_norm = arrive(r2n, bn_s, bn_r, own_n)
+    d_norm = own_n[...]
+    for peer in others:
+        at = place_of(*peer)
+        remote(r2n.at[at], r2n.at[at], bn_s.at[at], bn_r.at[at], sibling).wait_recv()
+        d_norm = d_norm + r2n[at].astype(F32)
     for peer in row_peers + col_peers:
-        home_copy(home_m, *peer).start()
+        home_half(*peer, 0).start()
     normal = scaled_ref[...]
     d_hat = d_norm * gain_ref[...]
     lead = jnp.mean(d_hat, axis=-1, keepdims=True)
@@ -375,6 +425,7 @@
     put(count + 1, everything, jnp.sum(d_norm, axis=0, keepdims=True))
     put(count + 2, everything, dscale[...] / scale_ref[...])
 
+    relay(0)
     @pl.loop(0, width // LANES)
     def _(c):
         lanes = lanes_of(c)
@@ -390,10 +441,14 @@
     s1_in = [remote(small.at[dp_peer(off)], ar1.at[dp_peer(off)], s1_s.at[off], s1_r.at[dp_peer(off)], sibling) for off in range(1, n_dp)]
     for copy in s1_out:
         copy.start()
+    for peer in row_peers + col_peers:
+        home_half(*peer, 1).start()
     for peer in diagonals:
-        home_copy(home_m, *peer).start()
+        for h in range(2):
+            home_half(*peer, h).start()
     ar1[d] = small[d]
 
+    relay(1)
     @pl.loop(0, width // LANES)
     def _(c):
         lanes = lanes_of(c)
@@ -409,22 +464,19 @@
     for copy in s2_out:
         copy.start()
 
-    halo_land(hg, halo_g, gpad)
-
-    @pl.loop(0, width // LANES)
-    def _(c):
-        lanes = lanes_of(c)
-        for i, value in convolve(gpad, True, lanes, far, {i: dfeat_ref[i, :, lanes] for i in far_rows}).items():
-            dfeat_ref[i, :, lanes] = value
-
     def owner_copy(which, b):
         return remote(fsend.at[which, b], frecv.at[which, place], fi_s.at[which, b], fi_r.at[which, place], (s * share + b, home))
 
-    for which in range(2):
+    def owner_send(which):
         total = gown[which]
         for off in range(1, n_sp):
-            plane_copy(which, off, True).wait_recv()
-            total = total + grecv[which, sp_peer(off)].astype(F32)
+            k = sp_peer(off)
+
+            @pl.when(jnp.logical_not(far_pair(k)))
+            def _():
+                plane_land(which, k)
+
+            total = total + grecv[which, k].astype(F32)
         for b in range(share):
             fsend[which, b] = total[b * part_rows:(b + 1) * part_rows].astype(BF16)
             pl.when(jnp.logical_not(is_self(b)))(owner_copy(which, b).start)
@@ -432,6 +484,9 @@
             @pl.when(is_self(b))
             def _():
                 frecv[which, b] = fsend[which, b]
+
+    owner_send(0)
+    owner_send(1)
 
     for copy in s2_in:
         copy.wait_recv()
@@ -441,7 +496,21 @@
     for copy in s3_out:
         copy.start()
 
-    mixed = arrive(r2m, bm_s, bm_r, own_m)
+    halo_land(hg, halo_g, gpad)
+
+    @pl.loop(0, width // LANES)
+    def _(c):
+        lanes = lanes_of(c)
+        for i, value in convolve(gpad, True, lanes, far, {i: dfeat_ref[i, :, lanes] for i in far_rows}).items():
+            dfeat_ref[i, :, lanes] = value
+
+    mixed = own_m[...]
+    for peer in others:
+        at = place_of(*peer)
+        for h in range(2):
+            span = pl.ds(h * half, half)
+            remote(r2m.at[at, span], r2m.at[at, span], bm_s.at[2 * at + h], bm_r.at[2 * at + h], sibling).wait_recv()
+        mixed = mixed + r2m[at].astype(F32)
     res_ref[...] = (x_ref[...].reshape(pixels, width).astype(F32) + scale_ref[...] * mixed).astype(BF16).reshape(rows, cols, width)
 
     for which, out in enumerate((gup_ref, gdown_ref)):
@@ -472,7 +541,7 @@
             copy.wait_send()
     for which in range(2):
         for off in range(1, n_sp):
-            plane_copy(which, off, False).wait_send()
+            plane_copy(which, sp_peer(off)).wait_send()
         for b in range(share):
             pl.when(jnp.logical_not(is_self(b)))(owner_copy(which, b).wait_send)
 
@@ -481,7 +550,8 @@
             swap_copy(which, k).wait_send()
     for peer in others:
         home_copy(home_n, *peer).wait_send()
-        home_copy(home_m, *peer).wait_send()
+        for h in range(2):
+            home_half(*peer, h).wait_send()
 
 
 def finish_kernel(*refs):
@@ -547,15 +617,15 @@
     ]
     scratch += [vm((2, n_sp, strip, hidden), BF16)] * 4
     scratch += [
-        vm((2, strip, hidden), F32),
+        vm((2, strip, hidden), F32), vm((2, strip, hidden), F32), vm((2, strip, hidden), BF16),
         vm((2, share, part_rows, hidden), BF16), vm((2, share, part_rows, hidden), BF16),
         vm((1, width), F32),
         vm((n_dp, per, width), F32), vm((n_dp, per, width), F32),
         vm((n_sp, per, width), F32), vm((n_dp, per, width), F32),
     ]
-    scratch += [dma(len(operands))] + [dma(2)] * 4 + [dma(n_dp)] * 2 + [dma(1)] * 2 + [dma(n_dp)] * 4 + [dma(chips)] * 4
+    scratch += [dma(len(operands))] + [dma(2)] * 4 + [dma(n_dp)] * 2 + [dma(1)] * 2 + [dma(n_dp)] * 4 + [dma(chips)] * 2 + [dma(n_dp)] * 2
     pair = lambda k: pltpu.SemaphoreType.DMA((2, k))
-    scratch += [pair(n_sp)] * 4 + [pair(share)] * 2 + [dma(n_dp)] * 2 + [dma(n_sp)] * 2 + [dma(n_dp)] * 2
+    scratch += [pair(n_sp)] * 4 + [dma(2)] + [pair(share)] * 2 + [dma(n_dp)] * 2 + [dma(n_sp)] * 2 + [dma(n_dp)] * 2
     outputs = pl.pallas_call(
         functools.partial(block_kernel, (n_dp, n_sp, rows, cols, width, taps)),
         out_shape=(

time: 47.5 us -> 44.6 us (0.939)
  Pallas kernels: 46.7 us -> 43.9 us
    pallas_call x1, Pallas kernels: 45.8 us -> 42.9 us  [local(): pl.pallas_call(functools.partial(block_kernel, (n_dp, n_sp, rows, cols, w...]
where the time goes in v3:
time: 44.6 us; the launch traced here: 44.5 us
  Pallas kernels  43.9 us (98%)
  between operations  0.64 us (1%)
    pallas_call x1, Pallas kernels, local(): pl.pallas_call(functools.partial(block_kernel, (n_dp, n_sp, rows, cols, w...  42.9 us
    pallas_call x1, Pallas kernels, finish(): pl.pallas_call(finish_kernel, out_shape=tuple((jax.ShapeDtypeStruct(a.sha...  0.94 us

profile of v3, /device:TPU:3, one launch (start us, length us, event | category | flops | bytes accessed | tf_op | source)
XLA Modules:
  0.0 44.5 jit_solution(1342333372702114133)
XLA Ops:
  0.6 42.9 %shard_map.143 = (bf16[8,16,512]{2,1,0:T(8,128)(2,1)S(1)}, f32[8,16,512]{2,1,0:T(8,128)S(1)}, f32[64,512]{1,0:T(8,128)S(1)}, f32[64,512]{1,0:T(8,128)S(1)}, f32[...) custom-call(bf16[8,16,512]{2,1,0:T(8,128)(2,1)} %bitcast.11, ...), custom_call_target="tpu_custom_call" | custom-call | tf_op jit(solution)/shard_map/pallas_call | solution.py:629
  43.6 0.9 %shard_map.144 = (bf16[8,16,512]{2,1,0:T(8,128)(2,1)}, f32[8,16,512]{2,1,0:T(8,128)}, f32[64,512]{1,0:T(8,128)}, f32[64,512]{1,0:T(8,128)}, f32[7,7,512]{2,1,0:T...) custom-call(bf16[8,16,512]{2,1,0:T(8,128)(2,1)S(1)} %get-tuple-element.24.refs_0_, ...), custom_call_target="tpu_custom_call" | custom-call | tf_op jit(solution)/shard_map/pallas_call | solution.py:567
